TPU v7x, 32 devices: a whole 2x2x4 slice. The times are simulated.
32 devices in a mesh: batch: 4 (over x, core), cache: 8 (over z, y).
Axes of the slice: x: 2, y: 2, z: 4, core: 2. Of those that a mesh axis runs over, the one named last changes fastest.
Arguments:
- arrivals: bfloat16 [16, 4, 4096], P('batch', None, 'cache'), may hold values from -6 to 6
- norm_gain: float32 [4096], replicated, may hold values from 0.25 to 1.75
- qkv_weight: bfloat16 [4096, 6144], P(None, 'cache'), may hold values from -0.09375 to 0.09375
- out_weight: bfloat16 [4096, 4096], P('cache'), may hold values from -0.09375 to 0.09375
- kv_cache: bfloat16 [16, 16, 2, 8, 128, 128], P('batch', 'cache'), as said below
- slot: int32 [16], replicated, may hold values from 0 to 15, each once
- positions: int32 [16], P('batch'), may hold values from 1664 to 2044
- tile_lists: int32 [16, 8], P('batch'), may hold values from 0 to 15, as said below
Outputs:
- attended: bfloat16 [16, 4, 4096], P('batch', None, 'cache')
Inputs may be any that keep to these rules, and one draw needn't show every extreme that they name: `tile_lists`: tiles of a row are distinct; the first is the tile of position positions - 1, the others lie at most 12 tiles before it. `kv_cache`: entries are of magnitude at most 240.
All inputs are finite; a program needn't handle non-finite values.
Results may differ from a plain program's by a relative error of at most 0.022.
Values may be sent and summed in bfloat16 or wider, within the bound.
A program may use at most 64 MiB of HBM per device.

v0:
```python
import math

import jax
import jax.numpy as jnp
from jax import lax
from jax.sharding import PartitionSpec as P

HEADS = 32
KVH = 8
HD = 128
TILE = 128
IMW = 64
CW = 16


epsilon = 1e-05
very_low = -1e30


def window_mask(query_pos, key_pos):
    return jnp.abs(key_pos % IMW - query_pos % IMW) <= CW


def shards(arrivals, norm_gain, qkv_weight, out_weight, kv_cache, slot, positions, tile_lists):
    row_count = positions.shape[0]
    step_count = arrivals.shape[1]
    groups = HEADS // KVH
    head_share = out_weight.shape[0] // HD
    head_start = lax.axis_index("cache") * head_share
    everyone = lax.all_gather(arrivals, "batch", axis=0, tiled=True)
    inverse = jnp.argsort(slot)
    my_rows = lax.dynamic_slice_in_dim(inverse, lax.axis_index("batch") * row_count, row_count)
    picked = jnp.take(everyone, my_rows, axis=0)
    whole = lax.all_gather(picked, "cache", axis=2, tiled=True)
    wide_values = whole.astype(jnp.float32)
    normed = (
        wide_values
        * lax.rsqrt(jnp.mean(wide_values * wide_values, axis=-1, keepdims=True) + epsilon)
        * norm_gain
    ).astype(jnp.bfloat16)
    projected = jnp.dot(
        normed.reshape(row_count * step_count, -1), qkv_weight, preferred_element_type=jnp.float32
    )
    projected = projected.astype(jnp.bfloat16).reshape(row_count, step_count, -1)
    heads_all = lax.all_gather(projected, "cache", axis=2, tiled=True).reshape(
        row_count, step_count, KVH, groups + 2, HD
    )
    queries = heads_all[:, :, :, :groups, :]
    new_keys = heads_all[:, :, :, groups, :]
    new_vals = heads_all[:, :, :, groups + 1, :]
    score_scale = 1.0 / math.sqrt(HD)
    tiles_here = kv_cache.shape[1]
    tile_ids = lax.axis_index("cache") * tiles_here + jnp.arange(tiles_here, dtype=jnp.int32)
    listed = jnp.any(tile_lists[:, :, None] == tile_ids[None, None, :], axis=1)
    key_pos = tile_ids[:, None] * TILE + jnp.arange(TILE, dtype=jnp.int32)[None, :]
    step_index = jnp.arange(step_count, dtype=jnp.int32)
    query_pos = positions[:, None] + step_index[None, :]
    key_valid = listed[:, None, :, None] & (key_pos[None, None] < positions[:, None, None, None])
    key_valid = key_valid & window_mask(query_pos[:, :, None, None], key_pos[None, None])
    valid_wide = key_valid[:, None, None]
    scores = (
        jnp.einsum(
            "bsjgd,btjkd->bjgstk", queries, kv_cache[:, :, 0], preferred_element_type=jnp.float32
        )
        * score_scale
    )
    new_valid = (step_index[None, :, None] >= step_index[None, None, :]) & window_mask(
        query_pos[:, :, None], query_pos[:, None, :]
    )
    new_scores = (
        jnp.einsum("bsjgd,bujd->bjgsu", queries, new_keys, preferred_element_type=jnp.float32)
        * score_scale
    )
    new_max = jnp.max(jnp.where(new_valid[:, None, None], new_scores, -jnp.inf), axis=-1)
    local_max = jnp.max(jnp.where(valid_wide, scores, very_low), axis=(-2, -1))
    values_here = kv_cache[:, :, 1]

    def own_heads(array):
        merged = array.reshape((row_count, HEADS) + array.shape[3:])
        return lax.dynamic_slice_in_dim(merged, head_start, head_share, 1)

    weights = jnp.where(valid_wide, jnp.exp(scores - local_max[..., None, None]), 0.0)
    totals = jnp.sum(weights, axis=(-2, -1))
    numerator = jnp.einsum(
        "bjgstk,btjkd->bjgsd",
        weights.astype(jnp.bfloat16),
        values_here,
        preferred_element_type=jnp.float32,
    )
    part_sums, part_totals, part_peaks = (
        lax.all_to_all(
            numerator.reshape(1, row_count, HEADS, step_count, HD).astype(jnp.bfloat16),
            "cache",
            split_axis=2,
            concat_axis=0,
            tiled=True,
        ).astype(jnp.float32),
        lax.all_to_all(
            totals.reshape(1, row_count, HEADS, step_count).astype(jnp.bfloat16),
            "cache",
            split_axis=2,
            concat_axis=0,
            tiled=True,
        ).astype(jnp.float32),
        lax.all_to_all(
            local_max.reshape(1, row_count, HEADS, step_count).astype(jnp.bfloat16),
            "cache",
            split_axis=2,
            concat_axis=0,
            tiled=True,
        ).astype(jnp.float32),
    )
    top_own = jnp.maximum(jnp.max(part_peaks, axis=0), own_heads(new_max))
    factor = jnp.exp(part_peaks - top_own[None])
    numer_own = jnp.sum(part_sums * factor[..., None], axis=0)
    total_own = jnp.sum(part_totals * factor, axis=0)
    own_new = own_heads(new_scores)
    new_weights = jnp.where(new_valid[:, None], jnp.exp(own_new - top_own[..., None]), 0.0)
    own_vals = lax.dynamic_slice_in_dim(
        jnp.repeat(new_vals, groups, axis=2), head_start, head_share, 2
    )
    total_all = total_own + jnp.sum(new_weights, axis=-1)
    numer_all = numer_own + jnp.einsum(
        "bhsu,buhd->bhsd",
        new_weights.astype(jnp.bfloat16),
        own_vals,
        preferred_element_type=jnp.float32,
    )
    attention = (numer_all / total_all[..., None]).astype(jnp.bfloat16)
    attn_flat = attention.transpose(0, 2, 1, 3).reshape(row_count * step_count, head_share * HD)
    partial_out = jnp.dot(attn_flat, out_weight, preferred_element_type=jnp.float32).reshape(
        row_count, step_count, -1
    )
    return lax.psum_scatter(
        partial_out.astype(jnp.bfloat16), "cache", scatter_dimension=2, tiled=True
    )


def solution(mesh):
    in_specs = (
        P("batch", None, "cache"),
        P(),
        P(None, "cache"),
        P("cache", None),
        P("batch", "cache", None, None, None, None),
        P(),
        P("batch"),
        P("batch", None),
    )
    out_specs = P("batch", None, "cache")
    return jax.shard_map(shards, mesh=mesh, in_specs=in_specs, out_specs=out_specs, check_vma=False)
```

profile of v0, /device:TPU:0, one launch (start us, length us, event | category | flops | bytes accessed | tf_op | source)
XLA Modules:
  0.0 208.3 jit_solution(18391242171131757612)
XLA Ops:
  6.5 0.9 compare_reduce_fusion
  7.5 0.7 add_select_fusion
  8.4 1.9 sort.17
  10.3 6.5 %all_gather.9 = bf16[16,4,512]{2,1,0:T(4,128)(2,1)S(1)} all-gather(bf16[4,4,512]{2,1,0:T(4,128)(2,1)} %param.8), channel_id=1, replica_groups=mesh['batch'=4,'cache'=8] {'batch'}, dimensions={0}, use_global_device_ids=true | all-gather | bytes 81920 | tf_op jit(solution)/shard_map/all_gather | solution.py:30
  16.8 0.6 gather_fusion
  17.5 31.3 %all_gather.10 = bf16[4,4,4096]{2,1,0:T(4,128)(2,1)S(1)} all-gather(bf16[4,4,512]{2,1,0:T(4,128)(2,1)S(1)} %broadcast_select_fusion), channel_id=1, replica_groups=mesh['batch'=4,'cache'=8] {'cache'}, dimensions={2}, use_global_device_ids=true | all-gather | bytes 147456 | tf_op jit(solution)/shard_map/all_gather | solution.py:34
  49.0 0.9 fusion.16
  49.9 3.7 %convolution_convert_fusion.1 = bf16[16,768]{1,0:T(8,128)(2,1)S(1)} fusion(bf16[16,4096]{1,0:T(8,128)(2,1)S(1)} %reshape.312, bf16[4096,768]{1,0:T(8,128)(2,1)} %param.10), kind=kOutput, calls=%fused_computation.13 | convolution fusion | flops 100675584 | bytes 6447104 | tf_op jit(solution)/shard_map/dot_general | solution.py:41
  53.6 30.7 %all_gather.11 = bf16[4,4,6144]{2,1,0:T(4,128)(2,1)S(1)} all-gather(bf16[4,4,768]{2,1,0:T(4,128)(2,1)S(1)} %reshape.313), channel_id=1, replica_groups=mesh['batch'=4,'cache'=8] {'cache'}, dimensions={2}, use_global_device_ids=true | all-gather | bytes 221184 | tf_op jit(solution)/shard_map/all_gather | solution.py:45
  84.5 2.6 %fusion.37 = (bf16[4,2,1,8,128,128]{5,4,3,2,1,0:T(8,128)(2,1)S(1)}, bf16[4,2,1,8,128,128]{5,4,3,2,1,0:T(8,128)(2,1)S(1)}) fusion(bf16[4,2,2,8,128,128]{5,4,3,2,1,0:T(8,128)(2,1)} %param.12), kind=kLoop, calls=%fused_computation.74 | loop fusion | bytes 8388608 | tf_op jit(solution)/shard_map/slice | solution.py:76
  87.4 0.8 select_reduce_fusion
  88.3 0.8 copy.116
  89.1 5.5 %all-to-all-start.1 = ((bf16[1,4,32,4]{3,1,0,2:T(4,128)(2,1)}), bf16[1,4,32,4]{3,1,0,2:T(4,128)(2,1)S(1)}, u32[]{:S(2)}, u32[]{:S(2)}) async-start(bf16[1,4,32,4]{3,1,0,2:T(4,128)(2,1)} %bitcast.15), calls=%async_computation.1 | async-start | bytes 65536 | tf_op jit(solution)/shard_map/all_to_all | solution.py:105
  94.8 0.5 fusion.12
  95.3 0.4 fusion.7
  95.7 1.3 select_reduce_fusion.1
  97.6 0.7 copy.94
  98.3 0.8 copy.120
  99.1 2.2 %all-to-all-done.1 = bf16[1,4,32,4]{3,1,0,2:T(4,128)(2,1)S(1)} async-done(((bf16[1,4,32,4]{3,1,0,2:T(4,128)(2,1)}), bf16[1,4,32,4]{3,1,0,2:T(4,128)(2,1)S(1)}, u32[]{:S(2)}, u32[]{:S(2)}) %all-to-all-start.1) | async-done | bytes 1056 | tf_op jit(solution)/shard_map/all_to_all | solution.py:105
  101.3 3.8 %all-to-all-start.2 = ((bf16[1,4,32,4]{3,1,0,2:T(4,128)(2,1)}), bf16[1,4,32,4]{3,1,0,2:T(4,128)(2,1)S(1)}, u32[]{:S(2)}, u32[]{:S(2)}) async-start(bf16[1,4,32,4]{3,1,0,2:T(4,128)(2,1)} %bitcast.26), calls=%async_computation.2 | async-start | bytes 65536 | tf_op jit(solution)/shard_map/all_to_all | solution.py:98
  105.1 0.3 copy.117
  105.4 6.3 %all-to-all-done.2 = bf16[1,4,32,4]{3,1,0,2:T(4,128)(2,1)S(1)} async-done(((bf16[1,4,32,4]{3,1,0,2:T(4,128)(2,1)}), bf16[1,4,32,4]{3,1,0,2:T(4,128)(2,1)S(1)}, u32[]{:S(2)}, u32[]{:S(2)}) %all-to-all-start.2) | async-done | bytes 1056 | tf_op jit(solution)/shard_map/all_to_all | solution.py:98
  111.8 3.4 %all-to-all-start = ((bf16[1,4,32,4,128]{4,3,1,0,2:T(4,128)(2,1)}), bf16[1,4,32,4,128]{4,3,1,0,2:T(4,128)(2,1)S(1)}, u32[]{:S(2)}, u32[]{:S(2)}) async-start(bf16[1,4,32,4,128]{4,3,1,0,2:T(4,128)(2,1)} %copy.94), calls=%async_computation | async-start | bytes 262144 | tf_op jit(solution)/shard_map/all_to_all | solution.py:91
  116.0 0.3 copy.101
  116.3 6.1 %all-to-all-done = bf16[1,4,32,4,128]{4,3,1,0,2:T(4,128)(2,1)S(1)} async-done(((bf16[1,4,32,4,128]{4,3,1,0,2:T(4,128)(2,1)}), bf16[1,4,32,4,128]{4,3,1,0,2:T(4,128)(2,1)S(1)}, u32[]{:S(2)}, u32[]{:S(2)}) %all-to-all-start) | async-done | bytes 131104 | tf_op jit(solution)/shard_map/all_to_all | solution.py:91
  122.4 0.2 fusion.17
  122.7 3.0 %convolution_convert_fusion = bf16[4,4,4096]{2,1,0:T(4,128)(2,1)S(1)} fusion(bf16[512,4096]{1,0:T(8,128)(2,1)} %param.11, bf16[4,4,4,4]{3,2,1,0:T(4,128)(2,1)S(1)} %copy.104, f32[4,4,4,128]{3,2,0,1:T(4,128)S(1)} %fusion.17, f32[4,4,4]{1,2,0:T(4,128)S(1)} %copy.110, bf16[4,4,32,128]{3,1,2,0:T(4,128)(2,1)S(1)} %bitcast.113, s32[]{:T(128)S(6)} %select_n.81), kind=kOutput, calls=%fused_computation.1 | convolution fusion | flops 67264512 | bytes 4399108 | tf_op jit(solution)/shard_map/dot_general | solution.py:131
  125.7 4.8 %copy.121 = bf16[4,4,4096]{1,0,2:T(4,128)(2,1)} copy(bf16[4,4,4096]{2,1,0:T(4,128)(2,1)S(1)} %convolution_convert_fusion) | data formatting | bytes 262144
  130.5 6.1 %reshape.338 = bf16[4096,16]{1,0:T(8,128)(2,1)} reshape(bf16[4096,4,4]{2,1,0:T(4,128)(2,1)} %bitcast.110) | data formatting | bytes 262144
  136.6 62.8 %reduce-scatter.4.cloned.1.call-done = bf16[512,16]{1,0:T(8,128)(2,1)} async-done(((bf16[4096,16]{1,0:T(8,128)(2,1)}), bf16[512,16]{1,0:T(8,128)(2,1)}) %reduce-scatter.4.cloned.1.call-update) | async-done | bytes 16400
  199.3 1.1 reshape.339
  200.5 0.9 copy.122
  (38 shorter events, 2.8 us)
Async XLA Ops:
  84.5 2.6 %copy-start = (s32[4]{0:T(128)S(1)}, s32[4]{0:T(128)}, u32[]{:S(2)}) copy-start(s32[4]{0:T(128)} %param.14) | copy-start | bytes 52
  89.1 12.2 %all-to-all-start.1 = ((bf16[1,4,32,4]{3,1,0,2:T(4,128)(2,1)}), bf16[1,4,32,4]{3,1,0,2:T(4,128)(2,1)S(1)}, u32[]{:S(2)}, u32[]{:S(2)}) async-start(bf16[1,4,32,4]{3,1,0,2:T(4,128)(2,1)} %bitcast.15), calls=%async_computation.1 | async-start | bytes 65536 | tf_op jit(solution)/shard_map/all_to_all | solution.py:105
  101.3 10.5 %all-to-all-start.2 = ((bf16[1,4,32,4]{3,1,0,2:T(4,128)(2,1)}), bf16[1,4,32,4]{3,1,0,2:T(4,128)(2,1)S(1)}, u32[]{:S(2)}, u32[]{:S(2)}) async-start(bf16[1,4,32,4]{3,1,0,2:T(4,128)(2,1)} %bitcast.26), calls=%async_computation.2 | async-start | bytes 65536 | tf_op jit(solution)/shard_map/all_to_all | solution.py:98
  111.8 10.7 %all-to-all-start = ((bf16[1,4,32,4,128]{4,3,1,0,2:T(4,128)(2,1)}), bf16[1,4,32,4,128]{4,3,1,0,2:T(4,128)(2,1)S(1)}, u32[]{:S(2)}, u32[]{:S(2)}) async-start(bf16[1,4,32,4,128]{4,3,1,0,2:T(4,128)(2,1)} %copy.94), calls=%async_computation | async-start | bytes 262144 | tf_op jit(solution)/shard_map/all_to_all | solution.py:91
  115.1 84.2 %reduce-scatter.4.cloned.1.call-start = ((), (), s32[]{:S(2)}) async-start(), calls=%async_computation.4 | async-start | bytes 1179648
Sparse Core Ops, SparseCore 0:
  136.7 62.6 reduce-scatter.3
where the time goes:
time: 209 us; the launch traced here: 208 us
  waiting for transfers between devices  77.5 us (37%)
  blocking collectives  68.5 us (33%)
  local copies, waits for them, and re-layouts  20.8 us (10%)
  between operations  13.6 us (7%)
  starting transfers between devices  12.7 us (6%)
  matrix products  9.2 us (4%)
  other arithmetic  6.06 us (3%)
    unnamed x2, waiting for transfers between devices  62.8 us
    all_gather x1, blocking collectives, shards(): whole = lax.all_gather(picked, 'cache', axis=2, tiled=True)  31.3 us
    all_gather x1, blocking collectives, shards(): lax.all_gather(projected, 'cache', axis=2, tiled=True)  30.7 us
    unnamed x6, local copies, waits for them, and re-layouts  12.9 us
    all_gather x1, blocking collectives, shards(): everyone = lax.all_gather(arrivals, 'batch', axis=0, tiled=True)  6.46 us
    all_to_all x1, waiting for transfers between devices, shards(): lax.all_to_all(totals.reshape(1, row_count, HEADS, step_count).astype(jnp...  6.33 us
    all_to_all x1, waiting for transfers between devices, shards(): lax.all_to_all(numerator.reshape(1, row_count, HEADS, step_count, HD).ast...  6.14 us
    all_to_all x1, starting transfers between devices, shards(): lax.all_to_all(local_max.reshape(1, row_count, HEADS, step_count).astype(...  5.49 us
  transfers between devices with their start and end apart: 4, of which 4 were waited for; matrix products, arithmetic and copies ran while one was open for 3% of the time, Pallas kernels for 0%

commit v1 on v0

--- a/solution.py
+++ b/solution.py
@@ -1,8 +1,11 @@
+import functools
 import math
 
 import jax
 import jax.numpy as jnp
 from jax import lax
+from jax.experimental import pallas as pl
+from jax.experimental.pallas import tpu as pltpu
 from jax.sharding import PartitionSpec as P
 
 HEADS = 32
@@ -17,32 +20,195 @@
 very_low = -1e30
 
 
+VMEM = pl.BlockSpec(memory_space=pltpu.VMEM)
+MESH = pl.DeviceIdType.MESH
+
+
+def greet(axis, size, me):
+    barrier = pltpu.get_barrier_semaphore()
+    for step in range(1, size):
+        pl.semaphore_signal(
+            barrier, inc=1, device_id={axis: lax.rem(me + step, size)}, device_id_type=MESH
+        )
+    pl.semaphore_wait(barrier, size - 1)
+
+
+def send(source, target, send_sem, recv_sem, axis, peer):
+    copy = pltpu.make_async_remote_copy(
+        src_ref=source,
+        dst_ref=target,
+        send_sem=send_sem,
+        recv_sem=recv_sem,
+        device_id={axis: peer},
+        device_id_type=MESH,
+    )
+    copy.start()
+    return copy
+
+
+def columns_of(index, width):
+    return pl.ds(pl.multiple_of(index * width, width), width)
+
+
+def communicate(kernel, out_shape, scratch, collective_id, *arrays):
+    count = len(out_shape) if isinstance(out_shape, tuple) else 0
+    return pl.pallas_call(
+        kernel,
+        out_shape=out_shape,
+        in_specs=[VMEM] * len(arrays),
+        out_specs=(VMEM,) * count if count else VMEM,
+        scratch_shapes=scratch,
+        compiler_params=pltpu.CompilerParams(collective_id=collective_id, has_side_effects=True),
+    )(*arrays)
+
+
+def gather_kernel(axis, size, on_columns, x_ref, out_ref, send_sems, recv_sems, own_sem):
+    me = lax.axis_index(axis)
+    if on_columns:
+        mine = out_ref.at[:, columns_of(me, x_ref.shape[1])]
+    else:
+        mine = out_ref.at[me]
+    own = pltpu.make_async_copy(x_ref, mine, own_sem)
+    own.start()
+    greet(axis, size, me)
+    copies = [
+        send(x_ref, mine, send_sems.at[k], recv_sems.at[k], axis, lax.rem(me + k, size))
+        for k in range(1, size)
+    ]
+    own.wait()
+    for copy in copies:
+        copy.wait()
+
+
+def gather(block, axis, size, on_columns, collective_id):
+    rows, width = block.shape
+    shape = (rows, size * width) if on_columns else (size, rows, width)
+    return communicate(
+        functools.partial(gather_kernel, axis, size, on_columns),
+        jax.ShapeDtypeStruct(shape, block.dtype),
+        [
+            pltpu.SemaphoreType.DMA((size,)),
+            pltpu.SemaphoreType.DMA((size,)),
+            pltpu.SemaphoreType.DMA,
+        ],
+        collective_id,
+        block,
+    )
+
+
+def swap_kernel(axis, size, a_ref, b_ref, a_out, b_out, send_sems, recv_sems, own_sems):
+    me = lax.axis_index(axis)
+    pairs = ((a_ref, a_out), (b_ref, b_out))
+    owns = []
+    for index, (source, target) in enumerate(pairs):
+        own = pltpu.make_async_copy(source.at[me], target.at[me], own_sems.at[index])
+        own.start()
+        owns.append(own)
+    greet(axis, size, me)
+    copies = []
+    for k in range(1, size):
+        peer = lax.rem(me + k, size)
+        for index, (source, target) in enumerate(pairs):
+            copies.append(
+                send(
+                    source.at[peer],
+                    target.at[me],
+                    send_sems.at[index, k],
+                    recv_sems.at[index, k],
+                    axis,
+                    peer,
+                )
+            )
+    for copy in owns + copies:
+        copy.wait()
+
+
+def swap(a, b, axis, size, collective_id):
+    return communicate(
+        functools.partial(swap_kernel, axis, size),
+        (jax.ShapeDtypeStruct(a.shape, a.dtype), jax.ShapeDtypeStruct(b.shape, b.dtype)),
+        [
+            pltpu.SemaphoreType.DMA((2, size)),
+            pltpu.SemaphoreType.DMA((2, size)),
+            pltpu.SemaphoreType.DMA((2,)),
+        ],
+        collective_id,
+        a,
+        b,
+    )
+
+
+def scatter_kernel(axis, size, x_ref, out_ref, held, send_sems, recv_sems):
+    me = lax.axis_index(axis)
+    width = out_ref.shape[1]
+    greet(axis, size, me)
+    copies = []
+    for k in range(1, size):
+        peer = lax.rem(me + k, size)
+        copies.append(
+            send(
+                x_ref.at[:, columns_of(peer, width)],
+                held.at[k],
+                send_sems.at[k],
+                recv_sems.at[k],
+                axis,
+                peer,
+            )
+        )
+    total = x_ref[:, columns_of(me, width)].astype(jnp.float32)
+    for k in range(1, size):
+        copies[k - 1].wait_recv()
+        total = total + held[k].astype(jnp.float32)
+    out_ref[...] = total.astype(out_ref.dtype)
+    for copy in copies:
+        copy.wait_send()
+
+
+def reduce_scatter(partial, axis, size, collective_id):
+    rows, width = partial.shape[0], partial.shape[1] // size
+    return communicate(
+        functools.partial(scatter_kernel, axis, size),
+        jax.ShapeDtypeStruct((rows, width), partial.dtype),
+        [
+            pltpu.VMEM((size, rows, width), partial.dtype),
+            pltpu.SemaphoreType.DMA((size,)),
+            pltpu.SemaphoreType.DMA((size,)),
+        ],
+        collective_id,
+        partial,
+    )
+
+
 def window_mask(query_pos, key_pos):
     return jnp.abs(key_pos % IMW - query_pos % IMW) <= CW
 
 
-def shards(arrivals, norm_gain, qkv_weight, out_weight, kv_cache, slot, positions, tile_lists):
+def shards(batch_size, cache_size, arrivals, norm_gain, qkv_weight, out_weight, kv_cache, slot, positions, tile_lists):
     row_count = positions.shape[0]
     step_count = arrivals.shape[1]
     groups = HEADS // KVH
     head_share = out_weight.shape[0] // HD
     head_start = lax.axis_index("cache") * head_share
-    everyone = lax.all_gather(arrivals, "batch", axis=0, tiled=True)
-    inverse = jnp.argsort(slot)
-    my_rows = lax.dynamic_slice_in_dim(inverse, lax.axis_index("batch") * row_count, row_count)
-    picked = jnp.take(everyone, my_rows, axis=0)
-    whole = lax.all_gather(picked, "cache", axis=2, tiled=True)
+    everyone = gather(
+        arrivals.reshape(row_count * step_count, -1), "batch", batch_size, False, 0
+    ).reshape(batch_size * row_count * step_count, -1)
+    my_row = lax.axis_index("batch") * row_count + jnp.arange(row_count * step_count) // step_count
+    my_step = jnp.arange(row_count * step_count) % step_count
+    their_row = jnp.repeat(slot, step_count)
+    their_step = jnp.arange(slot.shape[0] * step_count) % step_count
+    chosen = (my_row[:, None] == their_row[None]) & (my_step[:, None] == their_step[None])
+    picked = jnp.dot(
+        chosen.astype(jnp.bfloat16), everyone, preferred_element_type=jnp.float32
+    ).astype(jnp.bfloat16)
+    whole = gather(picked, "cache", cache_size, True, 1)
     wide_values = whole.astype(jnp.float32)
     normed = (
         wide_values
         * lax.rsqrt(jnp.mean(wide_values * wide_values, axis=-1, keepdims=True) + epsilon)
         * norm_gain
     ).astype(jnp.bfloat16)
-    projected = jnp.dot(
-        normed.reshape(row_count * step_count, -1), qkv_weight, preferred_element_type=jnp.float32
-    )
-    projected = projected.astype(jnp.bfloat16).reshape(row_count, step_count, -1)
-    heads_all = lax.all_gather(projected, "cache", axis=2, tiled=True).reshape(
+    projected = jnp.dot(normed, qkv_weight, preferred_element_type=jnp.float32)
+    heads_all = gather(projected.astype(jnp.bfloat16), "cache", cache_size, True, 2).reshape(
         row_count, step_count, KVH, groups + 2, HD
     )
     queries = heads_all[:, :, :, :groups, :]
@@ -87,29 +253,22 @@
         values_here,
         preferred_element_type=jnp.float32,
     )
-    part_sums, part_totals, part_peaks = (
-        lax.all_to_all(
-            numerator.reshape(1, row_count, HEADS, step_count, HD).astype(jnp.bfloat16),
-            "cache",
-            split_axis=2,
-            concat_axis=0,
-            tiled=True,
-        ).astype(jnp.float32),
-        lax.all_to_all(
-            totals.reshape(1, row_count, HEADS, step_count).astype(jnp.bfloat16),
-            "cache",
-            split_axis=2,
-            concat_axis=0,
-            tiled=True,
-        ).astype(jnp.float32),
-        lax.all_to_all(
-            local_max.reshape(1, row_count, HEADS, step_count).astype(jnp.bfloat16),
-            "cache",
-            split_axis=2,
-            concat_axis=0,
-            tiled=True,
-        ).astype(jnp.float32),
-    )
+    entries = row_count * head_share * step_count
+
+    def by_holder(array):
+        split = array.reshape((row_count, cache_size, head_share, step_count) + array.shape[4:])
+        return jnp.moveaxis(split, 1, 0)
+
+    sums_out = by_holder(numerator.astype(jnp.bfloat16)).reshape(cache_size, entries, HD)
+    stats_out = jnp.stack(
+        [by_holder(array).reshape(cache_size, entries) for array in (totals, local_max)], axis=1
+    )
+    stats_out = jnp.pad(stats_out, ((0, 0), (0, 6), (0, -entries % 128)))
+    part_sums, part_stats = swap(sums_out, stats_out, "cache", cache_size, 3)
+    kept = (cache_size, row_count, head_share, step_count)
+    part_sums = part_sums.reshape(kept + (HD,)).astype(jnp.float32)
+    part_totals = part_stats[:, 0, :entries].reshape(kept)
+    part_peaks = part_stats[:, 1, :entries].reshape(kept)
     top_own = jnp.maximum(jnp.max(part_peaks, axis=0), own_heads(new_max))
     factor = jnp.exp(part_peaks - top_own[None])
     numer_own = jnp.sum(part_sums * factor[..., None], axis=0)
@@ -128,11 +287,9 @@
     )
     attention = (numer_all / total_all[..., None]).astype(jnp.bfloat16)
     attn_flat = attention.transpose(0, 2, 1, 3).reshape(row_count * step_count, head_share * HD)
-    partial_out = jnp.dot(attn_flat, out_weight, preferred_element_type=jnp.float32).reshape(
+    partial_out = jnp.dot(attn_flat, out_weight, preferred_element_type=jnp.float32)
+    return reduce_scatter(partial_out.astype(jnp.bfloat16), "cache", cache_size, 4).reshape(
         row_count, step_count, -1
-    )
-    return lax.psum_scatter(
-        partial_out.astype(jnp.bfloat16), "cache", scatter_dimension=2, tiled=True
     )
 
 
@@ -148,4 +305,5 @@
         P("batch", None),
     )
     out_specs = P("batch", None, "cache")
-    return jax.shard_map(shards, mesh=mesh, in_specs=in_specs, out_specs=out_specs, check_vma=False)
+    body = functools.partial(shards, mesh.shape["batch"], mesh.shape["cache"])
+    return jax.shard_map(body, mesh=mesh, in_specs=in_specs, out_specs=out_specs, check_vma=False)

time: 209 us -> 74.6 us (0.36)
  waiting for transfers between devices: 77.5 us -> 0 us
  blocking collectives: 68.5 us -> 0 us
  Pallas kernels: 0 us -> 43.9 us
  between operations: 13.6 us -> 0.2 us
  starting transfers between devices: 12.7 us -> 0 us
  local copies, waits for them, and re-layouts: 20.8 us -> 10.4 us
  matrix products: 9.2 us -> 13.8 us
    all_gather x3 -> x0, blocking collectives: 68.5 us -> none  [the longest x1 31.3 us: shards(): whole = lax.all_gather(picked, 'cache', axis=2, tiled=True)]
    unnamed x2 -> x0, waiting for transfers between devices: 62.8 us -> none
    pallas_call x0 -> x5, Pallas kernels: none -> 43.9 us  [communicate(): pl.pallas_call(kernel, out_shape=out_shape, in_specs=[VMEM] * len(arrays)...]
    all_to_all x3 -> x0, waiting for transfers between devices: 14.7 us -> none  [the longest x1 6.33 us: shards(): lax.all_to_all(totals.reshape(1, row_count, HEADS, step_count).astype(jnp...]
    unnamed x6 -> x10, local copies, waits for them, and re-layouts: 12.9 us -> 0.02 us
    all_to_all x3 -> x0, starting transfers between devices: 12.6 us -> none  [the longest x1 5.49 us: shards(): lax.all_to_all(local_max.reshape(1, row_count, HEADS, step_count).astype(...]
    reshape x3, local copies, waits for them, and re-layouts: 0.27 us -> 3.15 us  [the longest x1 1.33 us: shards(): reduce_scatter(partial_out.astype(jnp.bfloat16), 'cache', cache_size, 4)]
    dot_general x1 -> x3, matrix products: 3.71 us -> 6.22 us  [the longest x1 4.43 us: shards(): projected = jnp.dot(normed, qkv_weight, preferred_element_type=jnp.float32)]
  transfers between devices with their start and end apart: 4 -> 0, of which waited for: 4 -> 0; matrix products, arithmetic and copies ran while one was open for 3% -> 0% of each run, Pallas kernels for 0% -> 0%
where the time goes in v1:
time: 74.6 us; the launch traced here: 73.9 us
  Pallas kernels  43.9 us (59%)
  matrix products  13.8 us (18%)
  local copies, waits for them, and re-layouts  10.4 us (14%)
  other arithmetic  5.67 us (8%)
    pallas_call x5, Pallas kernels, communicate(): pl.pallas_call(kernel, out_shape=out_shape, in_specs=[VMEM] * len(arrays)...  43.9 us
    dot_general x1, matrix products, shards(): projected = jnp.dot(normed, qkv_weight, preferred_element_type=jnp.float32)  4.43 us
    slice x1, local copies, waits for them, and re-layouts, shards(): kv_cache[:, :, 0]  4.23 us
    dot_general x1, matrix products, shards(): jnp.dot(attn_flat, out_weight, preferred_element_type=jnp.float32)  3.49 us
    dot_general x1, matrix products, shards(): jnp.einsum('bsjgd,btjkd->bjgstk', queries, kv_cache[:, :, 0], preferred_e...  2.35 us
    dot_general x1, matrix products, shards(): jnp.dot(chosen.astype(jnp.bfloat16), everyone, preferred_element_type=jnp...  1.64 us

profile of v1, /device:TPU:0, one launch (start us, length us, event | category | flops | bytes accessed | tf_op | source)
XLA Modules:
  0.0 73.9 jit_solution(6183070185678861693)
XLA Ops:
  0.0 4.2 %fusion.40 = (bf16[4,2,1,8,128,128]{5,4,3,2,1,0:T(8,128)(2,1)}, bf16[4,2,1,8,128,128]{5,4,3,2,1,0:T(8,128)(2,1)S(1)}) fusion(bf16[4,2,2,8,128,128]{5,4,3,2,1,0:T(8,128)(2,1)} %param.12), kind=kLoop, calls=%fused_computation.84 | loop fusion | bytes 8388608 | tf_op jit(solution)/shard_map/slice | solution.py:229
  4.2 0.2 compare_reduce_fusion
  4.9 0.6 reshape.303.x_ref
  5.5 6.3 %shard_map.82 = bf16[4,16,512]{2,1,0:T(8,128)(2,1)} custom-call(bf16[16,512]{1,0:T(8,128)(2,1)} %reshape.303.x_ref), custom_call_target="tpu_custom_call" | custom-call | tf_op jit(solution)/shard_map/pallas_call | solution.py:55
  12.0 1.6 %convolution_convert_fusion.2.x_ref = bf16[16,512]{1,0:T(8,128)(2,1)} fusion(bf16[64,512]{1,0:T(8,128)(2,1)} %bitcast.95, s32[64]{0:T(128)S(1)} %and_select_fusion, s32[64]{0:T(128)S(1)} %eq.57, s32[16]{0:T(128)S(1)} %get-tuple-element.27, s32[16]{0:T(128)S(1)} %get-tuple-element.28), kind=kOutput, calls=%fused_computation.17 | convolution fusion | flops 1059840 | bytes 82560 | tf_op jit(solution)/shard_map/dot_general | solution.py:200
  13.7 9.6 %shard_map.83 = bf16[16,4096]{1,0:T(8,128)(2,1)} custom-call(bf16[16,512]{1,0:T(8,128)(2,1)} %convolution_convert_fusion.2.x_ref), custom_call_target="tpu_custom_call" | custom-call | tf_op jit(solution)/shard_map/pallas_call | solution.py:55
  23.3 1.1 %fusion.13 = f32[16]{0:T(128)S(1)} fusion(bf16[16,4096]{1,0:T(8,128)(2,1)} %shard_map.83), kind=kLoop, calls=%fused_computation.24 | loop fusion | flops 196592 | bytes 131136 | tf_op jit(solution)/shard_map/reduce_sum | solution.py:207
  24.3 4.4 %convolution_convert_fusion.1.x_ref = bf16[16,768]{1,0:T(8,128)(2,1)} fusion(bf16[4096,768]{1,0:T(8,128)(2,1)} %param.10, bf16[16,4096]{1,0:T(8,128)(2,1)} %shard_map.83, f32[4096]{0:T(1024)S(1)} %copy-done, f32[16]{0:T(128)S(1)} %add_rsqrt_fusion), kind=kOutput, calls=%fused_computation.12 | convolution fusion | flops 100937728 | bytes 6463552 | tf_op jit(solution)/shard_map/dot_general | solution.py:210
  28.8 9.2 %shard_map.84 = bf16[16,6144]{1,0:T(8,128)(2,1)} custom-call(bf16[16,768]{1,0:T(8,128)(2,1)} %convolution_convert_fusion.1.x_ref), custom_call_target="tpu_custom_call" | custom-call | tf_op jit(solution)/shard_map/pallas_call | solution.py:55
  38.0 1.2 %reshape.305 = bf16[4,4,8,6,128]{4,3,2,1,0:T(8,128)(2,1)S(1)} reshape(bf16[16,6144]{1,0:T(8,128)(2,1)} %shard_map.84) | data formatting | bytes 393216 | tf_op jit(solution)/shard_map/reshape | solution.py:211
  39.2 2.4 %select_reduce_fusion = (f32[4,8,4,4]{2,3,1,0:T(4,128)S(1)}, f32[4,8,4,4,2,128]{5,2,4,3,1,0:T(4,128)S(1)}) fusion(pred[4,4,2,128]{3,2,1,0:T(4,128)(4,1)S(1)} %compare_and_fusion, bf16[4,2,1,8,128,128]{5,4,3,2,1,0:T(8,128)(2,1)} %get-tuple-element.9, bf16[4,4,8,6,128]{4,3,2,1,0:T(8,128)(2,1)S(1)} %reshape.305), kind=kOutput, calls=%fused_computation.19 | convolution fusion | flops 33947136 | bytes 2762752 | tf_op jit(solution)/shard_map/bsjgd,btjkd->bjgstk/dot_general | solution.py:228
  41.6 0.5 fusion.11
  42.1 0.4 fusion.7
  42.5 0.7 copy.72
  43.2 0.2 copy.74
  43.4 0.2 copy.73
  43.7 0.6 select_maximum_fusion.b_ref
  44.3 9.8 %shard_map.85 = (bf16[8,64,128]{2,1,0:T(8,128)(2,1)}, f32[8,8,128]{2,1,0:T(8,128)}) custom-call(bf16[8,64,128]{2,1,0:T(8,128)(2,1)} %bitcast.86, f32[8,8,128]{2,1,0:T(8,128)} %select_maximum_fusion.b_ref), custom_call_target="tpu_custom_call" | custom-call | tf_op jit(solution)/shard_map/pallas_call | solution.py:55
  54.1 0.8 %slice_reduce_fusion = f32[64]{0:T(128)S(1)} fusion(f32[8,8,128]{2,1,0:T(8,128)} %get-tuple-element.8), kind=kLoop, calls=%fused_computation.83 | loop fusion | flops 448 | bytes 2304 | tf_op jit(solution)/shard_map/reduce_max | solution.py:272
  55.1 0.1 fusion.41
  55.2 1.3 %select_reduce_fusion.1 = (f32[4,8,4,4]{2,3,1,0:T(4,128)S(1)}, f32[4,8,4,4,4]{2,4,3,1,0:T(4,128)S(1)}) fusion(pred[4,4,4]{2,1,0:T(4,128)(4,1)S(1)} %fusion.28, bf16[4,4,8,1,128]{4,3,2,1,0:T(2,128)(2,1)S(1)} %get-tuple-element.14, bf16[4,4,8,6,128]{4,3,2,1,0:T(8,128)(2,1)S(1)} %reshape.305), kind=kOutput, calls=%fused_computation.29 | convolution fusion | flops 529920 | bytes 208896 | tf_op jit(solution)/shard_map/bsjgd,bujd->bjgsu/dot_general | solution.py:237
  56.5 0.3 copy.92
  56.9 0.9 %multiply_reduce_fusion.1 = (f32[64]{0:T(128)S(1)}, f32[8,1,64]{2,1,0:T(1,128)S(1)}) fusion(f32[8,8,128]{2,1,0:T(8,128)} %get-tuple-element.8, f32[64]{0:T(128)S(1)} %sub.86), kind=kLoop, calls=%fused_computation.55 | loop fusion | flops 1472 | bytes 6656 | tf_op jit(solution)/shard_map/reduce_sum | solution.py:275
  57.8 1.0 %multiply_reduce_fusion = f32[64,128]{1,0:T(8,128)S(1)} fusion(bf16[8,64,128]{2,1,0:T(8,128)(2,1)} %get-tuple-element.7, f32[8,64]{1,0:T(8,128)S(1)} %subtract_exponential_fusion), kind=kLoop, calls=%fused_computation.28 | loop fusion | flops 188416 | bytes 165888 | tf_op jit(solution)/shard_map/reduce_sum | solution.py:274
  58.9 0.1 reshape.308
  59.2 0.1 fusion.23
  59.3 0.2 copy.83
  59.7 0.1 copy.85
  59.9 0.1 fusion.10
  60.1 3.5 %convolution_convert_fusion.x_ref = bf16[16,4096]{1,0:T(8,128)(2,1)} fusion(bf16[512,4096]{1,0:T(8,128)(2,1)} %param.11, bf16[2,8,4,128]{3,2,1,0:T(4,128)(2,1)S(1)} %bitcast.94), kind=kOutput, calls=%fused_computation | convolution fusion | flops 67174400 | bytes 4341760 | tf_op jit(solution)/shard_map/dot_general | solution.py:290
  63.6 9.0 %shard_map.86 = bf16[16,512]{1,0:T(8,128)(2,1)} custom-call(bf16[16,4096]{1,0:T(8,128)(2,1)} %convolution_convert_fusion.x_ref), custom_call_target="tpu_custom_call" | custom-call | tf_op jit(solution)/shard_map/pallas_call | solution.py:55
  72.6 1.3 %reshape.311 = bf16[4,4,512]{2,1,0:T(4,128)(2,1)} reshape(bf16[16,512]{1,0:T(8,128)(2,1)} %shard_map.86) | data formatting | bytes 32768 | tf_op jit(solution)/shard_map/reshape | solution.py:291
  (37 shorter events, 1.5 us)
Async XLA Ops:
  0.0 4.2 %copy-start.2 = (s32[4,8]{1,0:T(4,128)S(1)}, s32[4,8]{1,0:T(4,128)}, u32[]{:S(2)}) copy-start(s32[4,8]{1,0:T(4,128)} %param.15) | copy-start | bytes 388
  0.0 4.6 %copy-start.3 = (s32[4]{0:T(128)S(1)}, s32[4]{0:T(128)}, u32[]{:S(2)}) copy-start(s32[4]{0:T(128)} %param.14) | copy-start | bytes 52
  0.0 4.9 %copy-start.1 = (bf16[4,4,512]{2,1,0:T(4,128)(2,1)S(1)}, bf16[4,4,512]{2,1,0:T(4,128)(2,1)}, u32[]{:S(2)}) copy-start(bf16[4,4,512]{2,1,0:T(4,128)(2,1)} %param.8) | copy-start | bytes 49156
  0.0 11.8 %copy-start.4 = (s32[16]{0:T(128)S(1)}, s32[16]{0:T(128)}, u32[]{:S(2)}) copy-start(s32[16]{0:T(128)} %param.13) | copy-start | bytes 196
  0.0 24.3 %copy-start = (f32[4096]{0:T(1024)S(1)}, f32[4096]{0:T(1024)}, u32[]{:S(2)}) copy-start(f32[4096]{0:T(1024)} %param.9) | copy-start | bytes 49156
